TPU v7x, 32 devices: a whole 2x2x4 slice. The times are simulated.
32 devices in a mesh: rep: 2 (over x), ctx: 8 (over z, y), tp: 2 (over core).
Axes of the slice: x: 2, y: 2, z: 4, core: 2. Of those that a mesh axis runs over, the one named last changes fastest.
Arguments:
- queries: bfloat16 [4096, 4096], P(('rep', 'ctx'), 'tp'), parts along dimension 0, may hold values from -8 to 8
- rotated_key_rows: bfloat16 [4096, 512], P(('rep', 'ctx'), 'tp'), parts along dimension 0, may hold values from -8 to 8
- ordered_value_rows: bfloat16 [4096, 512], P(('rep', 'ctx'), 'tp'), parts along dimension 0, may hold values from -6 to 6
- block_order: int32 [32], P('rep'), parts along dimension 0, may hold values from 0 to 15, each once
- live_blocks: int32 [32, 12], P('rep'), parts along dimension 0, may hold values from -1 to 15, as said below
Outputs:
- attended: bfloat16 [4096, 4096], P(('rep', 'ctx', 'tp')), parts along dimension 0
- log_norm: float32 [64, 2048], P(('rep', 'tp'), 'ctx'), parts along dimension 0
There are 2 independent parts, one for each index of `rep`. A program takes and returns all parts, laid end to end along the dimension named above; each array names one. Nothing has to cross between parts.
Inputs may be any that keep to these rules, and one draw needn't show every extreme that they name: `live_blocks`: row s names block s in its first slot, then distinct blocks before s, then -1 in every unused slot; row 15 fills all 12 slots.
All inputs are finite; a program needn't handle non-finite values.
Results may differ from a plain program's by a relative error of at most 0.008.
Values may be sent and summed in bfloat16 or wider, within the bound.
A program may use at most 128 MiB of HBM per device.

v0:
```python
import jax
import jax.numpy as jnp
from jax import lax
from jax.sharding import PartitionSpec as P

HEAD_SIZE = 128
BLOCK_TOKENS = 128
NEG_LARGE = -1e30


def body(queries, rotated_key_rows, ordered_value_rows, block_order, live_blocks):
    tok_rows = queries.shape[0]
    kv_local = rotated_key_rows.shape[1] // HEAD_SIZE
    heads_local = queries.shape[1] // HEAD_SIZE
    query_groups = heads_local // kv_local
    blocks_total = block_order.shape[0]
    blocks_here = tok_rows // BLOCK_TOKENS
    factor = HEAD_SIZE ** (-0.5)
    shard_index = lax.axis_index("ctx")
    block_ids = jnp.arange(blocks_total, dtype=jnp.int32)
    my_blocks = lax.dynamic_slice_in_dim(block_order, shard_index * blocks_here, blocks_here)
    my_lists = jnp.take(live_blocks, my_blocks, axis=0)
    live_table = jnp.any(my_lists[:, :, None] == block_ids[None, None, :], axis=1)
    within = jnp.arange(BLOCK_TOKENS, dtype=jnp.int32)
    causal_square = within[None, :] <= within[:, None]
    query_heads = queries.reshape(tok_rows, kv_local, query_groups, HEAD_SIZE)
    carried = tuple(
        (
            (
                jnp.full((kv_local, query_groups, BLOCK_TOKENS), NEG_LARGE, jnp.float32),
                jnp.zeros((kv_local, query_groups, BLOCK_TOKENS), jnp.float32),
                jnp.zeros((kv_local, query_groups, BLOCK_TOKENS, HEAD_SIZE), jnp.float32),
            )
            for block_local in range(blocks_here)
        )
    )
    key_piece = lax.all_gather(rotated_key_rows, "ctx", axis=0, tiled=True)
    value_piece = lax.all_gather(ordered_value_rows, "ctx", axis=0, tiled=True)
    key_blocks = key_piece.shape[0] // BLOCK_TOKENS

    def one_key_block(turn_index, states):
        offset = turn_index * BLOCK_TOKENS
        key_part = lax.dynamic_slice_in_dim(key_piece, offset, BLOCK_TOKENS).reshape(
            BLOCK_TOKENS, kv_local, HEAD_SIZE
        )
        value_part = lax.dynamic_slice_in_dim(value_piece, offset, BLOCK_TOKENS).reshape(
            BLOCK_TOKENS, kv_local, HEAD_SIZE
        )
        key_seq = block_order[offset // BLOCK_TOKENS]
        updated = []
        for block_local in range(blocks_here):
            query_part = query_heads[block_local * BLOCK_TOKENS : (block_local + 1) * BLOCK_TOKENS]
            allowed = (key_seq != my_blocks[block_local]) | causal_square

            def compute_tile(current):
                running, denominator, weighted = current
                scores = (
                    jnp.einsum(
                        "qhgd,khd->hgqk", query_part, key_part, preferred_element_type=jnp.float32
                    )
                    * factor
                )
                scores = jnp.where(allowed, scores, NEG_LARGE)
                new_peak = jnp.maximum(running, jnp.max(scores, axis=-1))
                weights = jnp.where(allowed, jnp.exp(scores - new_peak[..., None]), 0.0)
                rescale = jnp.exp(running - new_peak)
                denominator = denominator * rescale + jnp.sum(weights, axis=-1)
                weighted = weighted * rescale[..., None] + jnp.einsum(
                    "hgqk,khd->hgqd",
                    weights.astype(jnp.bfloat16),
                    value_part,
                    preferred_element_type=jnp.float32,
                )
                return (new_peak, denominator, weighted)

            updated.append(
                lax.cond(
                    live_table[block_local, key_seq],
                    compute_tile,
                    lambda current: current,
                    states[block_local],
                )
            )
        return tuple(updated)

    states = lax.fori_loop(0, key_blocks, one_key_block, carried)
    running = jnp.concatenate([item[0] for item in states], axis=2)
    denominator = jnp.concatenate([item[1] for item in states], axis=2)
    weighted = jnp.concatenate([item[2] for item in states], axis=2)
    normed = weighted / denominator[..., None]
    merged_out = (
        jnp.transpose(normed, (2, 0, 1, 3))
        .reshape(tok_rows, heads_local * HEAD_SIZE)
        .astype(jnp.bfloat16)
    )
    log_norm = (running + jnp.log(denominator)).reshape(heads_local, tok_rows)
    attended = lax.all_to_all(merged_out, "tp", split_axis=0, concat_axis=1, tiled=True)
    return (attended, log_norm)


def solution(mesh):
    placed = (
        P(("rep", "ctx"), "tp"),
        P(("rep", "ctx"), "tp"),
        P(("rep", "ctx"), "tp"),
        P("rep"),
        P("rep", None),
    )
    return jax.shard_map(
        body,
        mesh=mesh,
        in_specs=placed,
        out_specs=(P(("rep", "ctx", "tp"), None), P(("rep", "tp"), "ctx")),
        check_vma=False,
    )
```

profile of v0, /device:TPU:0, one launch (start us, length us, event | category | flops | bytes accessed | tf_op | source)
XLA Modules:
  0.0 250.6 jit_solution(15988656583783142846)
XLA Ops:
  7.2 1.7 copy.39
  9.0 1.7 copy.40
  10.6 1.5 copy.41
  13.7 39.1 %all-gather.3.cloned.1.call-done = bf16[2048,256]{0,1:T(8,128)(2,1)} async-done(((bf16[256,256]{0,1:T(8,128)(2,1)}), bf16[2048,256]{0,1:T(8,128)(2,1)}) %all-gather.3.cloned.1.call-update) | async-done | bytes 1048592 | tf_op jit(solution)/shard_map/all_gather | solution.py:37
  52.8 40.5 %all-gather.5.cloned.1.call-done = bf16[2048,256]{0,1:T(8,128)(2,1)} async-done(((bf16[256,256]{0,1:T(8,128)(2,1)}), bf16[2048,256]{0,1:T(8,128)(2,1)}) %all-gather.5.cloned.1.call-update) | async-done | bytes 1048592 | tf_op jit(solution)/shard_map/all_gather | solution.py:38
  93.5 141.2 %while.27 = (s32[]{:T(128)}, f32[2,8,128]{2,1,0:T(8,128)S(1)}, f32[2,8,128]{2,1,0:T(8,128)S(1)}, f32[2,8,128,128]{3,2,1,0:T(8,128)S(1)}, f32[2,8,128]{2,1,0:T(8,...) while((s32[]{:T(128)}, f32[2,8,128]{2,1,0:T(8,128)S(1)}, ...), condition=%wide.region_10.11_spmd.clone.clone, body=%wide.region_1.10_spmd.clone.clone.sunk | while | flops 274260000 | bytes 12501754 | solution.py:86
  98.0 0.9 constant_dynamic-slice_fusion.7
  98.9 2.0 conditional.8
  100.2 0.7 convolution_add_fusion
  105.4 0.9 constant_dynamic-slice_fusion.7
  106.3 3.3 %conditional.9 = ((f32[2,8,128]{2,1,0:T(8,128)S(1)}, f32[2,8,128]{2,1,0:T(8,128)S(1)}, f32[2,8,128,128]{3,2,1,0:T(8,128)S(1)})) conditional(s32[]{:T(128)} %bitcast.60, (f32[2,8,128]{2,1,0:T(8,128)S(1)}, f32[2,8,128]{2,1,0:T(8,128)S(1)}, f32[2,8,128,128]{3,2,1,0:T(8,128)S(1)}) %tuple.96, (s32[2]{0:T(128)S(1)}, s32[]{:T(128)}, ...), branch_computations={%region_6.6_spmd, %region_7.9_spmd} | conditional | flops 137121792 | bytes 6111282 | solution.py:77
  114.2 0.9 constant_dynamic-slice_fusion.7
  115.0 2.0 conditional.8
  116.3 0.7 convolution_add_fusion
  117.1 3.3 %conditional.9 = ((f32[2,8,128]{2,1,0:T(8,128)S(1)}, f32[2,8,128]{2,1,0:T(8,128)S(1)}, f32[2,8,128,128]{3,2,1,0:T(8,128)S(1)})) conditional(s32[]{:T(128)} %bitcast.60, (f32[2,8,128]{2,1,0:T(8,128)S(1)}, f32[2,8,128]{2,1,0:T(8,128)S(1)}, f32[2,8,128,128]{3,2,1,0:T(8,128)S(1)}) %tuple.96, (s32[2]{0:T(128)S(1)}, s32[]{:T(128)}, ...), branch_computations={%region_6.6_spmd, %region_7.9_spmd} | conditional | flops 137121792 | bytes 6111282 | solution.py:77
  124.9 0.9 constant_dynamic-slice_fusion.7
  125.8 2.0 conditional.8
  127.8 3.3 %conditional.9 = ((f32[2,8,128]{2,1,0:T(8,128)S(1)}, f32[2,8,128]{2,1,0:T(8,128)S(1)}, f32[2,8,128,128]{3,2,1,0:T(8,128)S(1)})) conditional(s32[]{:T(128)} %bitcast.60, (f32[2,8,128]{2,1,0:T(8,128)S(1)}, f32[2,8,128]{2,1,0:T(8,128)S(1)}, f32[2,8,128,128]{3,2,1,0:T(8,128)S(1)}) %tuple.96, (s32[2]{0:T(128)S(1)}, s32[]{:T(128)}, ...), branch_computations={%region_6.6_spmd, %region_7.9_spmd} | conditional | flops 137121792 | bytes 6111282 | solution.py:77
  135.6 0.9 constant_dynamic-slice_fusion.7
  136.5 2.0 conditional.8
  138.5 3.3 %conditional.9 = ((f32[2,8,128]{2,1,0:T(8,128)S(1)}, f32[2,8,128]{2,1,0:T(8,128)S(1)}, f32[2,8,128,128]{3,2,1,0:T(8,128)S(1)})) conditional(s32[]{:T(128)} %bitcast.60, (f32[2,8,128]{2,1,0:T(8,128)S(1)}, f32[2,8,128]{2,1,0:T(8,128)S(1)}, f32[2,8,128,128]{3,2,1,0:T(8,128)S(1)}) %tuple.96, (s32[2]{0:T(128)S(1)}, s32[]{:T(128)}, ...), branch_computations={%region_6.6_spmd, %region_7.9_spmd} | conditional | flops 137121792 | bytes 6111282 | solution.py:77
  141.1 0.7 convolution_add_fusion.1
  146.3 0.9 constant_dynamic-slice_fusion.7
  147.2 2.0 conditional.8
  149.2 3.3 %conditional.9 = ((f32[2,8,128]{2,1,0:T(8,128)S(1)}, f32[2,8,128]{2,1,0:T(8,128)S(1)}, f32[2,8,128,128]{3,2,1,0:T(8,128)S(1)})) conditional(s32[]{:T(128)} %bitcast.60, (f32[2,8,128]{2,1,0:T(8,128)S(1)}, f32[2,8,128]{2,1,0:T(8,128)S(1)}, f32[2,8,128,128]{3,2,1,0:T(8,128)S(1)}) %tuple.96, (s32[2]{0:T(128)S(1)}, s32[]{:T(128)}, ...), branch_computations={%region_6.6_spmd, %region_7.9_spmd} | conditional | flops 137121792 | bytes 6111282 | solution.py:77
  157.0 0.9 constant_dynamic-slice_fusion.7
  162.5 0.9 constant_dynamic-slice_fusion.7
  163.4 3.3 %conditional.9 = ((f32[2,8,128]{2,1,0:T(8,128)S(1)}, f32[2,8,128]{2,1,0:T(8,128)S(1)}, f32[2,8,128,128]{3,2,1,0:T(8,128)S(1)})) conditional(s32[]{:T(128)} %bitcast.60, (f32[2,8,128]{2,1,0:T(8,128)S(1)}, f32[2,8,128]{2,1,0:T(8,128)S(1)}, f32[2,8,128,128]{3,2,1,0:T(8,128)S(1)}) %tuple.96, (s32[2]{0:T(128)S(1)}, s32[]{:T(128)}, ...), branch_computations={%region_6.6_spmd, %region_7.9_spmd} | conditional | flops 137121792 | bytes 6111282 | solution.py:77
  171.2 0.9 constant_dynamic-slice_fusion.7
  172.1 3.3 %conditional.9 = ((f32[2,8,128]{2,1,0:T(8,128)S(1)}, f32[2,8,128]{2,1,0:T(8,128)S(1)}, f32[2,8,128,128]{3,2,1,0:T(8,128)S(1)})) conditional(s32[]{:T(128)} %bitcast.60, (f32[2,8,128]{2,1,0:T(8,128)S(1)}, f32[2,8,128]{2,1,0:T(8,128)S(1)}, f32[2,8,128,128]{3,2,1,0:T(8,128)S(1)}) %tuple.96, (s32[2]{0:T(128)S(1)}, s32[]{:T(128)}, ...), branch_computations={%region_6.6_spmd, %region_7.9_spmd} | conditional | flops 137121792 | bytes 6111282 | solution.py:77
  179.9 0.9 constant_dynamic-slice_fusion.7
  180.8 2.0 conditional.8
  182.8 3.3 %conditional.9 = ((f32[2,8,128]{2,1,0:T(8,128)S(1)}, f32[2,8,128]{2,1,0:T(8,128)S(1)}, f32[2,8,128,128]{3,2,1,0:T(8,128)S(1)})) conditional(s32[]{:T(128)} %bitcast.60, (f32[2,8,128]{2,1,0:T(8,128)S(1)}, f32[2,8,128]{2,1,0:T(8,128)S(1)}, f32[2,8,128,128]{3,2,1,0:T(8,128)S(1)}) %tuple.96, (s32[2]{0:T(128)S(1)}, s32[]{:T(128)}, ...), branch_computations={%region_6.6_spmd, %region_7.9_spmd} | conditional | flops 137121792 | bytes 6111282 | solution.py:77
  190.6 0.9 constant_dynamic-slice_fusion.7
  191.5 2.0 conditional.8
  193.5 3.3 %conditional.9 = ((f32[2,8,128]{2,1,0:T(8,128)S(1)}, f32[2,8,128]{2,1,0:T(8,128)S(1)}, f32[2,8,128,128]{3,2,1,0:T(8,128)S(1)})) conditional(s32[]{:T(128)} %bitcast.60, (f32[2,8,128]{2,1,0:T(8,128)S(1)}, f32[2,8,128]{2,1,0:T(8,128)S(1)}, f32[2,8,128,128]{3,2,1,0:T(8,128)S(1)}) %tuple.96, (s32[2]{0:T(128)S(1)}, s32[]{:T(128)}, ...), branch_computations={%region_6.6_spmd, %region_7.9_spmd} | conditional | flops 137121792 | bytes 6111282 | solution.py:77
  201.4 0.9 constant_dynamic-slice_fusion.7
  206.8 0.9 constant_dynamic-slice_fusion.7
  207.7 3.3 %conditional.9 = ((f32[2,8,128]{2,1,0:T(8,128)S(1)}, f32[2,8,128]{2,1,0:T(8,128)S(1)}, f32[2,8,128,128]{3,2,1,0:T(8,128)S(1)})) conditional(s32[]{:T(128)} %bitcast.60, (f32[2,8,128]{2,1,0:T(8,128)S(1)}, f32[2,8,128]{2,1,0:T(8,128)S(1)}, f32[2,8,128,128]{3,2,1,0:T(8,128)S(1)}) %tuple.96, (s32[2]{0:T(128)S(1)}, s32[]{:T(128)}, ...), branch_computations={%region_6.6_spmd, %region_7.9_spmd} | conditional | flops 137121792 | bytes 6111282 | solution.py:77
  215.6 0.9 constant_dynamic-slice_fusion.7
  221.0 0.9 constant_dynamic-slice_fusion.7
  221.9 2.0 conditional.8
  228.5 0.9 constant_dynamic-slice_fusion.7
  229.4 2.0 conditional.8
  231.4 3.3 %conditional.9 = ((f32[2,8,128]{2,1,0:T(8,128)S(1)}, f32[2,8,128]{2,1,0:T(8,128)S(1)}, f32[2,8,128,128]{3,2,1,0:T(8,128)S(1)})) conditional(s32[]{:T(128)} %bitcast.60, (f32[2,8,128]{2,1,0:T(8,128)S(1)}, f32[2,8,128]{2,1,0:T(8,128)S(1)}, f32[2,8,128,128]{3,2,1,0:T(8,128)S(1)}) %tuple.96, (s32[2]{0:T(128)S(1)}, s32[]{:T(128)}, ...), branch_computations={%region_6.6_spmd, %region_7.9_spmd} | conditional | flops 137121792 | bytes 6111282 | solution.py:77
  234.7 0.7 fusion.27
  236.6 4.6 %all_to_all.16 = bf16[2,128,2048]{2,1,0:T(8,128)(2,1)S(1)} all-to-all(bf16[2,128,2048]{2,1,0:T(8,128)(2,1)S(1)} %convert_element_type.44), channel_id=1, replica_groups=mesh['rep'=2,'ctx'=8,'tp'=2] {'tp'}, dimensions={0} | all-to-all | bytes 2097152 | tf_op jit(solution)/shard_map/all_to_all | solution.py:97
  241.8 1.3 copy.45
  (234 shorter events, 55.3 us)
Async XLA Ops:
  7.2 5.8 %copy-start = (s32[16,12]{1,0:T(8,128)S(1)}, s32[16,12]{1,0:T(8,128)}, u32[]{:S(2)}) copy-start(s32[16,12]{1,0:T(8,128)} %param.15) | copy-start | bytes 2308
  7.2 45.6 %all-gather.3.cloned.1.call-start = ((), (), s32[]{:S(2)}) async-start(), calls=%async_computation.1 | async-start | bytes 1179648 | tf_op jit(solution)/shard_map/all_gather | solution.py:37
  8.9 84.3 %all-gather.5.cloned.1.call-start = ((), (), s32[]{:S(2)}) async-start(), calls=%async_computation.2 | async-start | bytes 1179648 | tf_op jit(solution)/shard_map/all_gather | solution.py:38
  12.1 0.7 copy-start.1
Sparse Core Ops, SparseCore 0:
  10.6 42.1 all-gather.2
  54.8 38.3 all-gather.4
where the time goes:
time: 253 us; the launch traced here: 251 us
  waiting for transfers between devices  79.6 us (31%)
  loops' own time  74.1 us (29%)
  local copies, waits for them, and re-layouts  50.8 us (20%)
  matrix products  21 us (8%)
  between operations  14.2 us (6%)
  other arithmetic  6.35 us (3%)
  blocking collectives  4.58 us (2%)
    another operation x1, loops' own time, body(): states = lax.fori_loop(0, key_blocks, one_key_block, carried)  52.4 us
    all_gather x1, waiting for transfers between devices, body(): value_piece = lax.all_gather(ordered_value_rows, 'ctx', axis=0, tiled=True)  40.5 us
    all_gather x1, waiting for transfers between devices, body(): key_piece = lax.all_gather(rotated_key_rows, 'ctx', axis=0, tiled=True)  39.1 us
    another operation x32, loops' own time, one_key_block(): lax.cond(live_table[block_local, key_seq], compute_tile, lambda current:...  21.7 us
    dynamic_slice x16, local copies, waits for them, and re-layouts, one_key_block(): lax.dynamic_slice_in_dim(value_piece, offset, BLOCK_TOKENS)  14.3 us
    dot_general x20, matrix products, compute_tile(): jnp.einsum('hgqk,khd->hgqd', weights.astype(jnp.bfloat16), value_part, pr...  13.7 us
    dynamic_slice x16, local copies, waits for them, and re-layouts, one_key_block(): live_table[block_local, key_seq]  10.6 us
    dynamic_slice x16, local copies, waits for them, and re-layouts, one_key_block(): key_seq = block_order[offset // BLOCK_TOKENS]  9.39 us
  transfers between devices with their start and end apart: 2, of which 2 were waited for; matrix products, arithmetic and copies ran while one was open for 2% of the time, Pallas kernels for 0%

commit v1 on v0

--- a/solution.py
+++ b/solution.py
@@ -6,6 +6,25 @@
 HEAD_SIZE = 128
 BLOCK_TOKENS = 128
 NEG_LARGE = -1e30
+
+
+def in_order(blocks, dim):
+    blocks = jnp.moveaxis(blocks, 0, dim)
+    lengths = blocks.shape
+    return blocks.reshape(*lengths[:dim], lengths[dim] * lengths[dim + 1], *lengths[dim + 2 :])
+
+
+def collected_by_bits(shard, axis):
+    size, index = (lax.axis_size(axis), lax.axis_index(axis))
+    blocks, stride = (shard[None], 1)
+    while stride < size:
+        received = lax.ppermute(blocks, axis, [(i, i ^ stride) for i in range(size)])
+        low = index & stride == 0
+        blocks = jnp.concatenate(
+            [jnp.where(low, blocks, received), jnp.where(low, received, blocks)]
+        )
+        stride *= 2
+    return blocks
 
 
 def body(queries, rotated_key_rows, ordered_value_rows, block_order, live_blocks):
@@ -34,7 +53,7 @@
             for block_local in range(blocks_here)
         )
     )
-    key_piece = lax.all_gather(rotated_key_rows, "ctx", axis=0, tiled=True)
+    key_piece = in_order(collected_by_bits(rotated_key_rows, "ctx"), 0)
     value_piece = lax.all_gather(ordered_value_rows, "ctx", axis=0, tiled=True)
     key_blocks = key_piece.shape[0] // BLOCK_TOKENS
 

time: 253 us -> 235 us (0.929)
  waiting for transfers between devices: 79.6 us -> 41.6 us
  local copies, waits for them, and re-layouts: 50.8 us -> 63.4 us
  starting transfers between devices: 0.08 us -> 7.49 us
  loops' own time: 74.1 us -> 70.6 us
  other arithmetic: 6.35 us -> 9.31 us
    all_gather x1 -> x0, waiting for transfers between devices: 39.1 us -> none  [body(): key_piece = lax.all_gather(rotated_key_rows, 'ctx', axis=0, tiled=True)]
    ppermute x0 -> x3, waiting for transfers between devices: none -> 30.1 us  [collected_by_bits(): lax.ppermute(blocks, axis, [(i, i ^ stride) for i in range(size)])]
    all_gather x1, waiting for transfers between devices: 40.5 us -> 11.5 us  [body(): value_piece = lax.all_gather(ordered_value_rows, 'ctx', axis=0, tiled=True)]
    dynamic_slice x0 -> x32, local copies, waits for them, and re-layouts: none -> 15.3 us  [one_key_block(): lax.dynamic_slice_in_dim(key_piece, offset, BLOCK_TOKENS)]
    ppermute x0 -> x3, starting transfers between devices: none -> 7.45 us  [collected_by_bits(): lax.ppermute(blocks, axis, [(i, i ^ stride) for i in range(size)])]
    unnamed x9 -> x8, local copies, waits for them, and re-layouts: 6.79 us -> 5.13 us
  transfers between devices with their start and end apart: 2 -> 4, of which waited for: 2 -> 4; matrix products, arithmetic and copies ran while one was open for 2% -> 3% of each run, Pallas kernels for 0% -> 0%
where the time goes in v1:
time: 235 us; the launch traced here: 232 us
  loops' own time  70.6 us (30%)
  local copies, waits for them, and re-layouts  63.4 us (27%)
  waiting for transfers between devices  41.6 us (18%)
  matrix products  21 us (9%)
  between operations  14.2 us (6%)
  other arithmetic  9.31 us (4%)
  starting transfers between devices  7.49 us (3%)
  blocking collectives  4.58 us (2%)
    another operation x1, loops' own time, body(): states = lax.fori_loop(0, key_blocks, one_key_block, carried)  50.5 us
    ppermute x3, waiting for transfers between devices, collected_by_bits(): lax.ppermute(blocks, axis, [(i, i ^ stride) for i in range(size)])  30.1 us
    another operation x32, loops' own time, one_key_block(): lax.cond(live_table[block_local, key_seq], compute_tile, lambda current:...  20.1 us
    dynamic_slice x32, local copies, waits for them, and re-layouts, one_key_block(): lax.dynamic_slice_in_dim(key_piece, offset, BLOCK_TOKENS)  15.3 us
    dot_general x20, matrix products, compute_tile(): jnp.einsum('hgqk,khd->hgqd', weights.astype(jnp.bfloat16), value_part, pr...  13.7 us
    dynamic_slice x16, local copies, waits for them, and re-layouts, one_key_block(): lax.dynamic_slice_in_dim(value_piece, offset, BLOCK_TOKENS)  13.6 us
    all_gather x1, waiting for transfers between devices, body(): value_piece = lax.all_gather(ordered_value_rows, 'ctx', axis=0, tiled=True)  11.5 us
    dynamic_slice x16, local copies, waits for them, and re-layouts, one_key_block(): live_table[block_local, key_seq]  10.6 us
  transfers between devices with their start and end apart: 4, of which 4 were waited for; matrix products, arithmetic and copies ran while one was open for 3% of the time, Pallas kernels for 0%

profile of v1, /device:TPU:0, one launch (start us, length us, event | category | flops | bytes accessed | tf_op | source)
XLA Modules:
  0.0 232.1 jit_solution(7165075657095704665)
XLA Ops:
  7.2 3.1 %collective-permute-start = (bf16[1,256,256]{2,1,0:T(8,128)(2,1)}, bf16[1,256,256]{2,1,0:T(8,128)(2,1)S(1)}, u32[]{:S(2)}, u32[]{:S(2)}) collective-permute-start(bf16[1,256,256]{2,1,0:T(8,128)(2,1)} %bitcast.77), channel_id=1, source_target_pairs={{0,2},{2,0},{4,6},{6,4},{8,10},{10,8},{12,14},{14,12},{1,3},{3,1},... | collective-permute-start | bytes 393224 | tf_op jit(solution)/shard_map/ppermute | solution.py:21
  10.3 1.7 copy.40
  12.0 2.0 collective-permute-done
  14.0 0.9 broadcast_select_fusion.5
  15.0 1.9 collective-permute-start.1
  16.9 5.6 %collective-permute-done.1 = bf16[2,256,256]{2,1,0:T(8,128)(2,1)S(1)} collective-permute-done((bf16[2,256,256]{2,1,0:T(8,128)(2,1)S(1)}, bf16[2,256,256]{2,1,0:T(8,128)(2,1)S(1)}, u32[]{:S(2)}, u32[]{:S(2)}) %collective-permute-start.1) | collective-permute-done | bytes 262176 | tf_op jit(solution)/shard_map/ppermute | solution.py:21
  23.4 2.5 %collective-permute-start.2 = (bf16[4,256,256]{2,1,0:T(8,128)(2,1)}, bf16[4,256,256]{2,1,0:T(8,128)(2,1)S(1)}, u32[]{:S(2)}, u32[]{:S(2)}) collective-permute-start(bf16[4,256,256]{2,1,0:T(8,128)(2,1)} %pad_maximum_fusion.1), channel_id=1, source_target_pairs={{0,8},{2,10},{4,12},{6,14},{8,0},{10,2},{12,4},{14,6},{1,9},{3,11}... | collective-permute-start | bytes 1572872 | tf_op jit(solution)/shard_map/ppermute | solution.py:21
  25.9 1.5 copy.41
  28.8 22.5 %collective-permute-done.2 = bf16[4,256,256]{2,1,0:T(8,128)(2,1)S(1)} collective-permute-done((bf16[4,256,256]{2,1,0:T(8,128)(2,1)}, bf16[4,256,256]{2,1,0:T(8,128)(2,1)S(1)}, u32[]{:S(2)}, u32[]{:S(2)}) %collective-permute-start.2) | collective-permute-done | bytes 524320 | tf_op jit(solution)/shard_map/ppermute | solution.py:21
  51.4 1.1 pad_maximum_fusion
  52.4 11.5 %all-gather.2.cloned.1.call-done = bf16[2048,256]{0,1:T(8,128)(2,1)} async-done(((bf16[256,256]{0,1:T(8,128)(2,1)}), bf16[2048,256]{0,1:T(8,128)(2,1)}) %all-gather.2.cloned.1.call-update) | async-done | bytes 1048592 | tf_op jit(solution)/shard_map/all_gather | solution.py:57
  64.1 152.1 %while.27 = (s32[]{:T(128)}, f32[2,8,128]{2,1,0:T(8,128)S(1)}, f32[2,8,128]{2,1,0:T(8,128)S(1)}, f32[2,8,128,128]{3,2,1,0:T(8,128)S(1)}, f32[2,8,128]{2,1,0:T(8,...) while((s32[]{:T(128)}, f32[2,8,128]{2,1,0:T(8,128)S(1)}, ...), condition=%wide.region_10.11_spmd.clone.clone, body=%wide.region_1.10_spmd.clone.clone.sunk | while | flops 274260000 | bytes 12632830 | solution.py:105
  68.5 0.9 constant_dynamic-slice_fusion.9
  70.4 2.0 conditional.8
  76.8 0.9 constant_dynamic-slice_fusion.9
  78.6 3.1 %conditional.9 = ((f32[2,8,128]{2,1,0:T(8,128)S(1)}, f32[2,8,128]{2,1,0:T(8,128)S(1)}, f32[2,8,128,128]{3,2,1,0:T(8,128)S(1)})) conditional(s32[]{:T(128)} %bitcast.64, (f32[2,8,128]{2,1,0:T(8,128)S(1)}, f32[2,8,128]{2,1,0:T(8,128)S(1)}, f32[2,8,128,128]{3,2,1,0:T(8,128)S(1)}) %tuple.96, (s32[2]{0:T(128)S(1)}, s32[]{:T(128)}, ...), branch_computations={%region_6.6_spmd, %region_7.9_spmd} | conditional | flops 137121792 | bytes 6111282 | solution.py:96
  86.1 0.9 constant_dynamic-slice_fusion.9
  88.0 2.0 conditional.8
  89.9 3.1 %conditional.9 = ((f32[2,8,128]{2,1,0:T(8,128)S(1)}, f32[2,8,128]{2,1,0:T(8,128)S(1)}, f32[2,8,128,128]{3,2,1,0:T(8,128)S(1)})) conditional(s32[]{:T(128)} %bitcast.64, (f32[2,8,128]{2,1,0:T(8,128)S(1)}, f32[2,8,128]{2,1,0:T(8,128)S(1)}, f32[2,8,128,128]{3,2,1,0:T(8,128)S(1)}) %tuple.96, (s32[2]{0:T(128)S(1)}, s32[]{:T(128)}, ...), branch_computations={%region_6.6_spmd, %region_7.9_spmd} | conditional | flops 137121792 | bytes 6111282 | solution.py:96
  97.5 0.9 constant_dynamic-slice_fusion.9
  99.3 2.0 conditional.8
  101.2 3.1 %conditional.9 = ((f32[2,8,128]{2,1,0:T(8,128)S(1)}, f32[2,8,128]{2,1,0:T(8,128)S(1)}, f32[2,8,128,128]{3,2,1,0:T(8,128)S(1)})) conditional(s32[]{:T(128)} %bitcast.64, (f32[2,8,128]{2,1,0:T(8,128)S(1)}, f32[2,8,128]{2,1,0:T(8,128)S(1)}, f32[2,8,128,128]{3,2,1,0:T(8,128)S(1)}) %tuple.96, (s32[2]{0:T(128)S(1)}, s32[]{:T(128)}, ...), branch_computations={%region_6.6_spmd, %region_7.9_spmd} | conditional | flops 137121792 | bytes 6111282 | solution.py:96
  108.8 0.9 constant_dynamic-slice_fusion.9
  110.6 2.0 conditional.8
  112.5 3.1 %conditional.9 = ((f32[2,8,128]{2,1,0:T(8,128)S(1)}, f32[2,8,128]{2,1,0:T(8,128)S(1)}, f32[2,8,128,128]{3,2,1,0:T(8,128)S(1)})) conditional(s32[]{:T(128)} %bitcast.64, (f32[2,8,128]{2,1,0:T(8,128)S(1)}, f32[2,8,128]{2,1,0:T(8,128)S(1)}, f32[2,8,128,128]{3,2,1,0:T(8,128)S(1)}) %tuple.96, (s32[2]{0:T(128)S(1)}, s32[]{:T(128)}, ...), branch_computations={%region_6.6_spmd, %region_7.9_spmd} | conditional | flops 137121792 | bytes 6111282 | solution.py:96
  120.1 0.9 constant_dynamic-slice_fusion.9
  121.9 2.0 conditional.8
  123.9 3.1 %conditional.9 = ((f32[2,8,128]{2,1,0:T(8,128)S(1)}, f32[2,8,128]{2,1,0:T(8,128)S(1)}, f32[2,8,128,128]{3,2,1,0:T(8,128)S(1)})) conditional(s32[]{:T(128)} %bitcast.64, (f32[2,8,128]{2,1,0:T(8,128)S(1)}, f32[2,8,128]{2,1,0:T(8,128)S(1)}, f32[2,8,128,128]{3,2,1,0:T(8,128)S(1)}) %tuple.96, (s32[2]{0:T(128)S(1)}, s32[]{:T(128)}, ...), branch_computations={%region_6.6_spmd, %region_7.9_spmd} | conditional | flops 137121792 | bytes 6111282 | solution.py:96
  131.4 0.9 constant_dynamic-slice_fusion.9
  137.7 0.9 constant_dynamic-slice_fusion.9
  139.5 3.1 %conditional.9 = ((f32[2,8,128]{2,1,0:T(8,128)S(1)}, f32[2,8,128]{2,1,0:T(8,128)S(1)}, f32[2,8,128,128]{3,2,1,0:T(8,128)S(1)})) conditional(s32[]{:T(128)} %bitcast.64, (f32[2,8,128]{2,1,0:T(8,128)S(1)}, f32[2,8,128]{2,1,0:T(8,128)S(1)}, f32[2,8,128,128]{3,2,1,0:T(8,128)S(1)}) %tuple.96, (s32[2]{0:T(128)S(1)}, s32[]{:T(128)}, ...), branch_computations={%region_6.6_spmd, %region_7.9_spmd} | conditional | flops 137121792 | bytes 6111282 | solution.py:96
  147.1 0.9 constant_dynamic-slice_fusion.9
  148.9 3.1 %conditional.9 = ((f32[2,8,128]{2,1,0:T(8,128)S(1)}, f32[2,8,128]{2,1,0:T(8,128)S(1)}, f32[2,8,128,128]{3,2,1,0:T(8,128)S(1)})) conditional(s32[]{:T(128)} %bitcast.64, (f32[2,8,128]{2,1,0:T(8,128)S(1)}, f32[2,8,128]{2,1,0:T(8,128)S(1)}, f32[2,8,128,128]{3,2,1,0:T(8,128)S(1)}) %tuple.96, (s32[2]{0:T(128)S(1)}, s32[]{:T(128)}, ...), branch_computations={%region_6.6_spmd, %region_7.9_spmd} | conditional | flops 137121792 | bytes 6111282 | solution.py:96
  156.4 0.9 constant_dynamic-slice_fusion.9
  158.3 2.0 conditional.8
  160.2 3.1 %conditional.9 = ((f32[2,8,128]{2,1,0:T(8,128)S(1)}, f32[2,8,128]{2,1,0:T(8,128)S(1)}, f32[2,8,128,128]{3,2,1,0:T(8,128)S(1)})) conditional(s32[]{:T(128)} %bitcast.64, (f32[2,8,128]{2,1,0:T(8,128)S(1)}, f32[2,8,128]{2,1,0:T(8,128)S(1)}, f32[2,8,128,128]{3,2,1,0:T(8,128)S(1)}) %tuple.96, (s32[2]{0:T(128)S(1)}, s32[]{:T(128)}, ...), branch_computations={%region_6.6_spmd, %region_7.9_spmd} | conditional | flops 137121792 | bytes 6111282 | solution.py:96
  167.8 0.9 constant_dynamic-slice_fusion.9
  169.6 2.0 conditional.8
  171.5 3.1 %conditional.9 = ((f32[2,8,128]{2,1,0:T(8,128)S(1)}, f32[2,8,128]{2,1,0:T(8,128)S(1)}, f32[2,8,128,128]{3,2,1,0:T(8,128)S(1)})) conditional(s32[]{:T(128)} %bitcast.64, (f32[2,8,128]{2,1,0:T(8,128)S(1)}, f32[2,8,128]{2,1,0:T(8,128)S(1)}, f32[2,8,128,128]{3,2,1,0:T(8,128)S(1)}) %tuple.96, (s32[2]{0:T(128)S(1)}, s32[]{:T(128)}, ...), branch_computations={%region_6.6_spmd, %region_7.9_spmd} | conditional | flops 137121792 | bytes 6111282 | solution.py:96
  179.1 0.9 constant_dynamic-slice_fusion.9
  185.4 0.9 constant_dynamic-slice_fusion.9
  187.2 3.1 %conditional.9 = ((f32[2,8,128]{2,1,0:T(8,128)S(1)}, f32[2,8,128]{2,1,0:T(8,128)S(1)}, f32[2,8,128,128]{3,2,1,0:T(8,128)S(1)})) conditional(s32[]{:T(128)} %bitcast.64, (f32[2,8,128]{2,1,0:T(8,128)S(1)}, f32[2,8,128]{2,1,0:T(8,128)S(1)}, f32[2,8,128,128]{3,2,1,0:T(8,128)S(1)}) %tuple.96, (s32[2]{0:T(128)S(1)}, s32[]{:T(128)}, ...), branch_computations={%region_6.6_spmd, %region_7.9_spmd} | conditional | flops 137121792 | bytes 6111282 | solution.py:96
  194.7 0.9 constant_dynamic-slice_fusion.9
  202.9 2.0 conditional.8
  211.1 2.0 conditional.8
  213.1 3.1 %conditional.9 = ((f32[2,8,128]{2,1,0:T(8,128)S(1)}, f32[2,8,128]{2,1,0:T(8,128)S(1)}, f32[2,8,128,128]{3,2,1,0:T(8,128)S(1)})) conditional(s32[]{:T(128)} %bitcast.64, (f32[2,8,128]{2,1,0:T(8,128)S(1)}, f32[2,8,128]{2,1,0:T(8,128)S(1)}, f32[2,8,128,128]{3,2,1,0:T(8,128)S(1)}) %tuple.96, (s32[2]{0:T(128)S(1)}, s32[]{:T(128)}, ...), branch_computations={%region_6.6_spmd, %region_7.9_spmd} | conditional | flops 137121792 | bytes 6111282 | solution.py:96
  218.1 4.6 %all_to_all.16 = bf16[2,128,2048]{2,1,0:T(8,128)(2,1)S(1)} all-to-all(bf16[2,128,2048]{2,1,0:T(8,128)(2,1)S(1)} %convert_element_type.44), channel_id=1, replica_groups=mesh['rep'=2,'ctx'=8,'tp'=2] {'tp'}, dimensions={0} | all-to-all | bytes 2097152 | tf_op jit(solution)/shard_map/all_to_all | solution.py:116
  223.3 1.3 copy.45
  (274 shorter events, 75.7 us)
Async XLA Ops:
  7.2 20.9 %copy-start = (s32[16,12]{1,0:T(8,128)S(1)}, s32[16,12]{1,0:T(8,128)}, u32[]{:S(2)}) copy-start(s32[16,12]{1,0:T(8,128)} %param.15) | copy-start | bytes 2308
  7.2 9.7 %copy-start.1 = (s32[16]{0:T(128)S(1)}, s32[16]{0:T(128)}, u32[]{:S(2)}) copy-start(s32[16]{0:T(128)} %param.14) | copy-start | bytes 196
  7.2 56.7 %all-gather.2.cloned.1.call-start = ((), (), s32[]{:S(2)}) async-start(), calls=%async_computation.1 | async-start | bytes 1179648 | tf_op jit(solution)/shard_map/all_gather | solution.py:57
  7.2 6.8 %collective-permute-start = (bf16[1,256,256]{2,1,0:T(8,128)(2,1)}, bf16[1,256,256]{2,1,0:T(8,128)(2,1)S(1)}, u32[]{:S(2)}, u32[]{:S(2)}) collective-permute-start(bf16[1,256,256]{2,1,0:T(8,128)(2,1)} %bitcast.77), channel_id=1, source_target_pairs={{0,2},{2,0},{4,6},{6,4},{8,10},{10,8},{12,14},{14,12},{1,3},{3,1},... | collective-permute-start | bytes 393224 | tf_op jit(solution)/shard_map/ppermute | solution.py:21
  15.0 7.5 %collective-permute-start.1 = (bf16[2,256,256]{2,1,0:T(8,128)(2,1)S(1)}, bf16[2,256,256]{2,1,0:T(8,128)(2,1)S(1)}, u32[]{:S(2)}, u32[]{:S(2)}) collective-permute-start(bf16[2,256,256]{2,1,0:T(8,128)(2,1)S(1)} %pad_maximum_fusion.2), channel_id=1, source_target_pairs={{0,4},{2,6},{4,0},{6,2},{8,12},{10,14},{12,8},{14,10},{1,5},{3,7},... | collective-permute-start | bytes 786440 | tf_op jit(solution)/shard_map/ppermute | solution.py:21
  23.4 27.9 %collective-permute-start.2 = (bf16[4,256,256]{2,1,0:T(8,128)(2,1)}, bf16[4,256,256]{2,1,0:T(8,128)(2,1)S(1)}, u32[]{:S(2)}, u32[]{:S(2)}) collective-permute-start(bf16[4,256,256]{2,1,0:T(8,128)(2,1)} %pad_maximum_fusion.1), channel_id=1, source_target_pairs={{0,8},{2,10},{4,12},{6,14},{8,0},{10,2},{12,4},{14,6},{1,9},{3,11}... | collective-permute-start | bytes 1572872 | tf_op jit(solution)/shard_map/ppermute | solution.py:21
Sparse Core Ops, SparseCore 0:
  12.1 51.7 all-gather.1
